TPU v7x, 128 devices: a whole 4x4x4 slice. The times are simulated.
128 devices in a mesh: dp: 16 (over y, x), head: 8 (over z, core).
Axes of the slice: x: 4, y: 4, z: 4, core: 2. Of those that a mesh axis runs over, the one named last changes fastest.
Arguments:
- slot_token_ids: int32 [128, 512], P('dp'), may hold values from 0 to 50264
- lengths: int32 [128], P('dp'), may hold values from 64 to 512, as said below
- labels: int32 [128], P('dp'), may hold values from 0 to 2
- optimizer_step_count: int32 [], replicated, may hold values from 2 to 20
- token_embedding_table: bfloat16 [50304, 1024], P('dp', 'head'), may hold values from -6 to 6
- positions: bfloat16 [512, 1024], replicated, may hold values from -4 to 4
- query_key_value_weight: bfloat16 [3, 1024, 1024], P(None, None, 'head'), may hold values from -0.1875 to 0.1875
- attention_output_weight: bfloat16 [1024, 1024], P('head'), may hold values from -0.8 to 0.8
- feedforward_input_weight: bfloat16 [1024, 4096], P(None, 'head'), may hold values from -0.1875 to 0.1875
- feedforward_output_weight: bfloat16 [4096, 1024], P('head'), may hold values from -0.09375 to 0.09375
- layer_norm_gains: float32 [3, 1024], replicated, may hold values from 0.5 to 1.5
- layer_norm_biases: float32 [3, 1024], replicated, may hold values from -2 to 2
- classifier: bfloat16 [3, 1024], replicated, may hold values from -0.75 to 0.75
- adapter_down_maps: float32 [2, 1024, 16], replicated, may hold values from -0.1875 to 0.1875
- adapter_up_maps: float32 [2, 16, 1024], P(None, None, 'head'), may hold values from -1.5 to 1.5
- down_first_moment: float32 [2, 1024, 16], P(None, 'dp'), may hold values from -0.0078125 to 0.0078125
- down_second_moment: float32 [2, 1024, 16], P(None, 'dp'), may hold values from 2.1972657e-08 to 9.1552735e-08
- up_first_moment: float32 [2, 16, 1024], P(None, None, ('head', 'dp')), may hold values from -0.0078125 to 0.0078125
- up_second_moment: float32 [2, 16, 1024], P(None, None, ('head', 'dp')), may hold values from 2.1972657e-08 to 9.1552735e-08
- down_privacy_noise: float32 [2, 1024, 16], P(None, 'dp'), may hold values from -6 to 6
- up_privacy_noise: float32 [2, 16, 1024], P(None, None, ('head', 'dp')), may hold values from -6 to 6
Outputs:
- loss: float32 [], replicated
- example_norms: float32 [128], P(('dp', 'head'))
- a_moment1: float32 [2, 1024, 16], P(None, 'dp')
- a_moment2: float32 [2, 1024, 16], P(None, 'dp')
- a_weight: float32 [2, 1024, 16], P(None, 'dp')
- b_moment1: float32 [2, 16, 1024], P(None, None, ('head', 'dp'))
- b_moment2: float32 [2, 16, 1024], P(None, None, ('head', 'dp'))
- b_weight: float32 [2, 16, 1024], P(None, None, ('head', 'dp'))
- lamb_norms: float32 [4, 2], replicated
Inputs may be any that keep to these rules, and one draw needn't show every extreme that they name: `lengths`: valid tokens of each example; some example has exactly 512.
All inputs are finite; a program needn't handle non-finite values.
Results may differ from a plain program's by a relative error of at most 0.0059.
Values may be sent and summed in bfloat16 or wider, within the bound.
No kernel may reach another device: no remote copies, remote signals or barrier semaphores. Data moves between devices by JAX's collectives and lax.ppermute only.
A program may use at most 256 MiB of HBM per device.

v0:
```python
import jax
import jax.numpy as jnp
from jax import lax
from jax.sharding import PartitionSpec as P

HDIM = 64
MICRO = 4
precise = lax.Precision.HIGHEST
adapter_scale = 2.0
clip_bound = 1.0
noise_mult = 0.6
smooth_rate = 0.1
beta_one = 0.9
beta_two = 0.999
adam_eps = 1e-06
decay_rate = 0.01
learn_rate = 0.25
norm_eps = 1e-05
contract_last = (((1,), (1,)), ((), ()))


def gelu_exact(inputs):
    return jax.nn.gelu(inputs, approximate=False)


def norm_rows(inputs, gain, bias):
    centre = inputs - jnp.mean(inputs, -1, keepdims=True)
    inv_std = lax.rsqrt(jnp.mean(centre * centre, -1, keepdims=True) + norm_eps)
    return (centre * inv_std * gain + bias, inv_std)


def norm_back(grad, normed, inv_std, gain, bias):
    x_hat = (normed - bias) / gain
    scaled = grad * gain
    return inv_std * (
        scaled
        - jnp.mean(scaled, -1, keepdims=True)
        - x_hat * jnp.mean(scaled * x_hat, -1, keepdims=True)
    )


def branch_add(partial_out, resid, gain, bias):
    total = lax.psum(partial_out, "head")
    return norm_rows(resid + total, gain, bias)


def masked_scores(query_h, key_h, valid_mask):
    scores = jnp.einsum(
        "eqhd,ekhd->ehqk", query_h, key_h, preferred_element_type=jnp.float32
    ) * HDIM ** (-0.5)
    return jnp.where(valid_mask[:, None, None, :], scores, -1e30)


def layer_forward(
    hidden_initial, valid_mask, length_float, class_label, frozen_params, adapter_reduced
):
    w_qkv, w_o, w_in, w_out, gains, biases, class_w = frozen_params
    down_pair, up_reduced = adapter_reduced
    example_count, sequence_length = valid_mask.shape
    width = hidden_initial.shape[1]
    local_w = w_o.shape[0]
    adapter_width = up_reduced.shape[1]
    shape4 = (example_count, sequence_length, local_w // HDIM, HDIM)
    hidden_reduced = hidden_initial.astype(jnp.bfloat16)
    adapter_activation = jnp.dot(
        hidden_reduced, down_pair, preferred_element_type=jnp.float32
    ).astype(jnp.bfloat16)
    query_low = (
        (
            jnp.dot(hidden_reduced, w_qkv[0], preferred_element_type=jnp.float32)
            + adapter_scale
            * jnp.dot(
                adapter_activation[:, :adapter_width],
                up_reduced[0],
                preferred_element_type=jnp.float32,
            )
        )
        .astype(jnp.bfloat16)
        .reshape(shape4)
    )
    key_low = (
        jnp.dot(hidden_reduced, w_qkv[1], preferred_element_type=jnp.float32)
        .astype(jnp.bfloat16)
        .reshape(shape4)
    )
    value_low = (
        (
            jnp.dot(hidden_reduced, w_qkv[2], preferred_element_type=jnp.float32)
            + adapter_scale
            * jnp.dot(
                adapter_activation[:, adapter_width:],
                up_reduced[1],
                preferred_element_type=jnp.float32,
            )
        )
        .astype(jnp.bfloat16)
        .reshape(shape4)
    )
    scores = masked_scores(query_low, key_low, valid_mask)
    row_top = jnp.max(scores, -1, keepdims=True)
    log_total = row_top + jnp.log(jnp.sum(jnp.exp(scores - row_top), -1, keepdims=True))
    attn_prob = jnp.exp(scores - log_total)
    context = (
        jnp.einsum(
            "ehqk,ekhd->eqhd",
            attn_prob.astype(jnp.bfloat16),
            value_low,
            preferred_element_type=jnp.float32,
        )
        .astype(jnp.bfloat16)
        .reshape(-1, local_w)
    )
    hidden_one, std_one = branch_add(
        jnp.dot(context, w_o, preferred_element_type=jnp.float32),
        hidden_initial,
        gains[1],
        biases[1],
    )
    ffn_pre = jnp.dot(hidden_one.astype(jnp.bfloat16), w_in, preferred_element_type=jnp.float32)
    ffn_part = jnp.dot(
        gelu_exact(ffn_pre).astype(jnp.bfloat16), w_out, preferred_element_type=jnp.float32
    )
    hidden_two, std_two = branch_add(ffn_part, hidden_one, gains[2], biases[2])
    valid_f = valid_mask.astype(jnp.float32)
    pooled = (
        jnp.sum(hidden_two.reshape(example_count, sequence_length, width) * valid_f[..., None], 1)
        / length_float[:, None]
    )
    logits = lax.dot_general(
        pooled.astype(jnp.bfloat16), class_w, contract_last, preferred_element_type=jnp.float32
    )
    log_prob = jax.nn.log_softmax(logits, -1)
    target = (1.0 - smooth_rate) * jax.nn.one_hot(
        class_label, class_w.shape[0], dtype=jnp.float32
    ) + smooth_rate / class_w.shape[0]
    losses = -jnp.sum(target * log_prob, -1)
    d_logit = jnp.exp(log_prob) - target
    d_pooled = jnp.dot(d_logit, class_w.astype(jnp.float32), precision=precise)
    d_two = (d_pooled[:, None, :] * (valid_f / length_float[:, None])[..., None]).reshape(-1, width)
    d_sum_two = norm_back(d_two, hidden_two, std_two, gains[2], biases[2])
    grad_act = lax.dot_general(
        d_sum_two.astype(jnp.bfloat16), w_out, contract_last, preferred_element_type=jnp.float32
    )
    d_pre = jax.vjp(gelu_exact, ffn_pre)[1](grad_act)[0].astype(jnp.bfloat16)
    back_part = lax.dot_general(d_pre, w_in, contract_last, preferred_element_type=jnp.float32)
    d_one = d_sum_two + lax.psum(back_part, "head")
    d_attn = norm_back(d_one, hidden_one, std_one, gains[1], biases[1]).astype(jnp.bfloat16)
    d_context = (
        lax.dot_general(d_attn, w_o, contract_last, preferred_element_type=jnp.float32)
        .astype(jnp.bfloat16)
        .reshape(shape4)
    )
    attn_prob = jnp.exp(masked_scores(query_low, key_low, valid_mask) - log_total)
    d_value = jnp.einsum(
        "ehqk,eqhd->ekhd",
        attn_prob.astype(jnp.bfloat16),
        d_context,
        preferred_element_type=jnp.float32,
    ).astype(jnp.bfloat16)
    d_prob = jnp.einsum("eqhd,ekhd->ehqk", d_context, value_low, preferred_element_type=jnp.float32)
    d_score = (attn_prob * (d_prob - jnp.sum(attn_prob * d_prob, -1, keepdims=True))).astype(
        jnp.bfloat16
    )
    d_query = (
        jnp.einsum("ehqk,ekhd->eqhd", d_score, key_low, preferred_element_type=jnp.float32)
        * HDIM ** (-0.5)
    ).astype(jnp.bfloat16)
    dq_rows = d_query.reshape(-1, local_w)
    dv_rows = d_value.reshape(-1, local_w)
    example_activation = adapter_activation.reshape(
        example_count, sequence_length, 2 * adapter_width
    )
    up_gradient = adapter_scale * jnp.stack(
        [
            jnp.einsum(
                "elr,eld->erd",
                example_activation[..., :adapter_width],
                dq_rows.reshape(example_count, sequence_length, local_w),
                preferred_element_type=jnp.float32,
            ),
            jnp.einsum(
                "elr,eld->erd",
                example_activation[..., adapter_width:],
                dv_rows.reshape(example_count, sequence_length, local_w),
                preferred_element_type=jnp.float32,
            ),
        ],
        1,
    )
    inner_portion = adapter_scale * jnp.concatenate(
        [
            lax.dot_general(
                dq_rows, up_reduced[0], contract_last, preferred_element_type=jnp.float32
            ),
            lax.dot_general(
                dv_rows, up_reduced[1], contract_last, preferred_element_type=jnp.float32
            ),
        ],
        1,
    )
    inner_full = lax.psum(inner_portion, "head")
    inner_sum = inner_full.astype(jnp.bfloat16)
    grad_both = jnp.einsum(
        "eld,elr->edr",
        hidden_reduced.reshape(example_count, sequence_length, width),
        inner_sum.reshape(example_count, sequence_length, 2 * adapter_width),
        preferred_element_type=jnp.float32,
    )
    down_gradient = jnp.stack([grad_both[..., :adapter_width], grad_both[..., adapter_width:]], 1)
    return (losses, down_gradient, up_gradient)


def apply_blocks(hidden_rows, lengths, labels, frozen_params, adapter_reduced, encoder_block):
    example_count, sequence_length, width = hidden_rows.shape
    valid_all = jnp.arange(sequence_length)[None, :] < lengths[:, None]
    loss_list, down_list, up_list = ([], [], [])
    for block_idx in range(example_count // encoder_block):
        first_ex = block_idx * encoder_block
        last_ex = first_ex + encoder_block
        losses, down_gradient, up_gradient = layer_forward(
            hidden_rows[first_ex:last_ex].reshape(-1, width),
            valid_all[first_ex:last_ex],
            lengths[first_ex:last_ex].astype(jnp.float32),
            labels[first_ex:last_ex],
            frozen_params,
            adapter_reduced,
        )
        loss_list.append(losses)
        down_list.append(down_gradient)
        up_list.append(up_gradient)
    return (
        jnp.concatenate(loss_list, 0),
        jnp.concatenate(down_list, 0),
        jnp.concatenate(up_list, 0),
    )


def lamb_direction(weight, grad, first, second, step_number):
    first_new = beta_one * first + (1.0 - beta_one) * grad
    second_new = beta_two * second + (1.0 - beta_two) * grad * grad
    direction = (
        first_new
        / (1.0 - jnp.power(beta_one, step_number))
        / (jnp.sqrt(second_new / (1.0 - jnp.power(beta_two, step_number))) + adam_eps)
        + decay_rate * weight
    )
    return (first_new, second_new, direction)


def per_device(
    slot_token_ids,
    lengths,
    labels,
    optimizer_step_count,
    token_embedding_table,
    positions,
    query_key_value_weight,
    attention_output_weight,
    feedforward_input_weight,
    feedforward_output_weight,
    layer_norm_gains,
    layer_norm_biases,
    classifier,
    adapter_down_maps,
    adapter_up_maps,
    down_first_moment,
    down_second_moment,
    up_first_moment,
    up_second_moment,
    down_privacy_noise,
    up_privacy_noise,
):
    n_head = lax.axis_size("head")
    dataset_size = lax.axis_size("dp")
    ex_dev, sequence_length = slot_token_ids.shape
    width = positions.shape[1]
    every_ids = lax.all_gather(slot_token_ids, "dp", axis=0, tiled=True).reshape(-1)
    vocab_local = token_embedding_table.shape[0]
    offset = lax.axis_index("dp") * vocab_local
    ids_here = every_ids - offset
    inside = (ids_here >= 0) & (ids_here < vocab_local)
    picked = jnp.take(token_embedding_table, jnp.clip(ids_here, 0, vocab_local - 1), axis=0)
    columns = lax.psum_scatter(
        jnp.where(inside[:, None], picked.astype(jnp.float32), 0.0).astype(jnp.bfloat16),
        "dp",
        scatter_dimension=0,
        tiled=True,
    )
    pos_f = positions.astype(jnp.float32)[None]
    down_reduced = adapter_down_maps.astype(jnp.bfloat16)
    down_pair = jnp.concatenate([down_reduced[0], down_reduced[1]], 1)
    micro_examples = ex_dev // MICRO
    own_share = ex_dev // n_head
    tokens = lax.all_gather(columns, "head", axis=1, tiled=True)
    hidden_all, unused_std = norm_rows(
        tokens.astype(jnp.float32).reshape(ex_dev, sequence_length, width) + pos_f,
        layer_norm_gains[0],
        layer_norm_biases[0],
    )
    frozen_params = (
        query_key_value_weight,
        attention_output_weight,
        feedforward_input_weight,
        feedforward_output_weight,
        layer_norm_gains,
        layer_norm_biases,
        classifier,
    )
    losses, grads_down, grads_up = apply_blocks(
        hidden_all,
        lengths,
        labels,
        frozen_params,
        (down_pair, adapter_up_maps.astype(jnp.bfloat16)),
        micro_examples,
    )
    part_sums = jnp.sum(grads_down * grads_down, (1, 2, 3)) / n_head + jnp.sum(
        grads_up * grads_up, (1, 2, 3)
    )
    arrived = lax.all_to_all(
        part_sums.reshape(n_head, own_share), "head", split_axis=0, concat_axis=0, tiled=True
    )
    example_norms = jnp.sqrt(jnp.sum(arrived, 0))
    own_factor = clip_bound / jnp.maximum(example_norms, clip_bound)
    factors = lax.all_gather(own_factor, "head", axis=0, tiled=True)
    sum_down = jnp.einsum("e,eabc->abc", factors, grads_down, precision=precise)
    sum_up = jnp.einsum("e,eabc->abc", factors, grads_up, precision=precise)
    loss_part = jnp.sum(losses) / n_head
    red_down, red_up = (
        lax.psum_scatter(sum_down, "dp", scatter_dimension=1, tiled=True),
        lax.psum_scatter(sum_up, "dp", scatter_dimension=2, tiled=True),
    )
    examples = ex_dev * dataset_size
    down_gradient = (red_down + noise_mult * clip_bound * down_privacy_noise) / examples
    up_gradient = (red_up + noise_mult * clip_bound * up_privacy_noise) / examples
    step_number = optimizer_step_count.astype(jnp.float32)
    down_rows = adapter_down_maps.shape[1] // dataset_size
    down_weight = lax.dynamic_slice_in_dim(
        adapter_down_maps, lax.axis_index("dp") * down_rows, down_rows, 1
    )
    up_columns = adapter_up_maps.shape[2] // dataset_size
    up_weight = lax.dynamic_slice_in_dim(
        adapter_up_maps, lax.axis_index("dp") * up_columns, up_columns, 2
    )
    down_momentum, down_velocity, dir_down = lamb_direction(
        down_weight, down_gradient, down_first_moment, down_second_moment, step_number
    )
    up_momentum, up_velocity, dir_up = lamb_direction(
        up_weight, up_gradient, up_first_moment, up_second_moment, step_number
    )
    sq_down = (
        jnp.stack(
            [jnp.sum(down_weight * down_weight, (1, 2)), jnp.sum(dir_down * dir_down, (1, 2))], 1
        )
        / n_head
    )
    sq_up = jnp.stack([jnp.sum(up_weight * up_weight, (1, 2)), jnp.sum(dir_up * dir_up, (1, 2))], 1)
    total_down, total_up, loss_sum = lax.psum((sq_down, sq_up, loss_part), ("dp", "head"))
    norm_table = jnp.sqrt(jnp.concatenate([total_down, total_up], 0))
    updated_down = (
        down_weight - learn_rate * (norm_table[:2, 0] / norm_table[:2, 1])[:, None, None] * dir_down
    )
    updated_up = (
        up_weight - learn_rate * (norm_table[2:, 0] / norm_table[2:, 1])[:, None, None] * dir_up
    )
    return (
        loss_sum / examples,
        example_norms,
        down_momentum,
        down_velocity,
        updated_down,
        up_momentum,
        up_velocity,
        updated_up,
        norm_table,
    )


def solution(mesh):
    placed = (
        P("dp", None),
        P("dp"),
        P("dp"),
        P(),
        P("dp", "head"),
        P(),
        P(None, None, "head"),
        P("head", None),
        P(None, "head"),
        P("head", None),
        P(),
        P(),
        P(),
        P(),
        P(None, None, "head"),
        P(None, "dp", None),
        P(None, "dp", None),
        P(None, None, ("head", "dp")),
        P(None, None, ("head", "dp")),
        P(None, "dp", None),
        P(None, None, ("head", "dp")),
    )
    return jax.shard_map(
        per_device,
        mesh=mesh,
        in_specs=placed,
        out_specs=(
            P(),
            P(("dp", "head")),
            P(None, "dp", None),
            P(None, "dp", None),
            P(None, "dp", None),
            P(None, None, ("head", "dp")),
            P(None, None, ("head", "dp")),
            P(None, None, ("head", "dp")),
            P(),
        ),
        check_vma=False,
    )
```

profile of v0, /device:TPU:1, one launch (start us, length us, event | category | flops | bytes accessed | tf_op | source)
XLA Modules:
  0.0 1647.0 jit_solution(5846328891770936799)
XLA Ops:
  7.3 19.8 %all_gather.9 = s32[128,512]{1,0:T(8,128)S(1)} all-gather(s32[8,512]{1,0:T(8,128)} %param.22), channel_id=1, replica_groups=mesh['dp'=16,'head'=8] {'dp'}, dimensions={0}, use_global_device_ids=true | all-gather | bytes 278528 | tf_op jit(solution)/shard_map/all_gather | solution.py:277
  28.1 229.0 %gather_fusion = bf16[65536,128]{1,0:T(8,128)(2,1)} fusion(bf16[3144,128]{1,0:T(8,128)(2,1)S(1)} %copy-done.1, s32[65536]{0:T(1024)S(1)} %broadcast_clamp_fusion), kind=kCustom, calls=%fused_computation | custom fusion | bytes 33816576 | tf_op jit(solution)/shard_map/jit(_take)/gather | solution.py:282
  257.0 46.3 %select_convert_fusion = bf16[65536,128]{1,0:T(8,128)(2,1)} fusion(bf16[65536,128]{1,0:T(8,128)(2,1)} %gather_fusion, pred[65536]{0:T(1024)(128)(4,1)S(1)} %compare_and_fusion, pred[65536]{0:T(1024)(128)(4,1)S(1)} %bitcast.555), kind=kLoop, calls=%fused_computation.1 | loop fusion | flops 33554432 | bytes 33685504 | tf_op jit(solution)/shard_map/convert_element_type | solution.py:284
  303.4 115.6 %reduce-scatter.6.cloned.1.call-done = bf16[4096,128]{1,0:T(8,128)(2,1)} async-done(((bf16[65536,128]{1,0:T(8,128)(2,1)}), bf16[4096,128]{1,0:T(8,128)(2,1)}) %reduce-scatter.6.cloned.1.call-update) | async-done | bytes 1048592 | tf_op jit(solution)/shard_map/reduce_scatter | solution.py:283
  423.8 51.6 %all-gather.2.cloned.1.call-done = bf16[4096,1024]{1,0:T(8,128)(2,1)} async-done(((bf16[4096,128]{1,0:T(8,128)(2,1)}), bf16[4096,1024]{1,0:T(8,128)(2,1)}) %all-gather.2.cloned.1.call-update) | async-done | bytes 8388624 | tf_op jit(solution)/shard_map/all_gather | solution.py:294
  475.4 5.1 fusion
  480.5 5.9 multiply_reduce_fusion
  486.4 6.1 multiply_add_fusion
  492.5 3.6 fusion.384
  496.1 4.8 fusion.383
  501.0 3.9 fusion.183
  565.9 3.3 fusion.135
  574.0 3.3 fusion.133
  580.3 183.9 %all-reduce.15.cloned.1.call-done = (f32[1024,1024]{1,0:T(8,128)}, f32[1024,1024]{1,0:T(8,128)}, f32[1024,1024]{1,0:T(8,128)}, f32[1024,1024]{1,0:T(8,128)}) async-done(((f32[1024,1024]{1,0:T(8,128)}, f32[1024,1024]{1,0:T(8,128)}, f32[1024,1024]{1,0:T(8,128)}, f32[1024,1024]{1,0:T(8,128)}), (f32[1024,1024]{1,0:T(8,128)}, f32[1024,1024]{1,0:T(8,128)}, f32[1024,1024]{1,0:T(8,128)}, ...) | async-done | bytes 16777232 | tf_op jit(solution)/shard_map/psum | solution.py:43
  764.3 4.1 fusion.382
  769.0 3.2 copy-done.31
  777.6 6.8 fusion.140
  784.4 6.7 fusion.138
  794.9 6.7 fusion.139
  806.8 6.7 fusion.137
  814.4 183.4 %all-reduce.13.cloned.1.call-done = (f32[1024,1024]{1,0:T(8,128)}, f32[1024,1024]{1,0:T(8,128)}, f32[1024,1024]{1,0:T(8,128)}, f32[1024,1024]{1,0:T(8,128)}) async-done(((f32[1024,1024]{1,0:T(8,128)}, f32[1024,1024]{1,0:T(8,128)}, f32[1024,1024]{1,0:T(8,128)}, f32[1024,1024]{1,0:T(8,128)}), (f32[1024,1024]{1,0:T(8,128)}, f32[1024,1024]{1,0:T(8,128)}, f32[1024,1024]{1,0:T(8,128)}, ...) | async-done | bytes 16777232 | tf_op jit(solution)/shard_map/psum | solution.py:43
  997.8 12.3 fusion.371
  1012.7 4.3 multiply_reduce_fusion.13
  1019.7 5.7 fusion.24
  1027.7 8.9 fusion.18
  1036.7 10.9 fusion.144
  1047.5 3.9 fusion.31
  1051.4 11.0 fusion.143
  1062.5 7.4 fusion.29
  1069.8 10.8 fusion.142
  1080.6 10.9 fusion.141
  1102.5 173.5 %all-reduce.11.cloned.1.call-done = (f32[1024,1024]{1,0:T(8,128)}, f32[1024,1024]{1,0:T(8,128)}, f32[1024,1024]{1,0:T(8,128)}, f32[1024,1024]{1,0:T(8,128)}) async-done(((f32[1024,1024]{1,0:T(8,128)}, f32[1024,1024]{1,0:T(8,128)}, f32[1024,1024]{1,0:T(8,128)}, f32[1024,1024]{1,0:T(8,128)}), (f32[1024,1024]{1,0:T(8,128)}, f32[1024,1024]{1,0:T(8,128)}, f32[1024,1024]{1,0:T(8,128)}, ...) | async-done | bytes 16777232 | tf_op jit(solution)/shard_map/psum | solution.py:146
  1276.0 7.9 fusion.370
  1286.7 3.5 convolution_convert_fusion
  1295.3 5.9 fusion.369
  1304.0 3.5 convolution_convert_fusion.1
  1307.6 3.5 multiply_reduce_fusion.4
  1312.6 5.9 fusion.368
  1321.4 3.5 convolution_convert_fusion.2
  1324.9 3.6 multiply_reduce_fusion.7
  1330.0 5.9 fusion.367
  1338.7 3.5 convolution_convert_fusion.3
  1359.7 29.7 %all-reduce.16 = (bf16[1024,32]{0,1:T(8,128)(2,1)}, bf16[1024,32]{0,1:T(8,128)(2,1)}, bf16[1024,32]{0,1:T(8,128)(2,1)}, bf16[1024,32]{0,1:T(8,128)(2,1)}) all-reduce(f32[1024,32]{0,1:T(8,128)S(1)} %maximum_multiply_fusion.3, f32[1024,32]{0,1:T(8,128)} %maximum_multiply_fusion.2, ...), channel_id=1, replica_groups=mesh['dp'=16,'head'=8] {'head'}, use_global_device_ids=true, to_apply=%region_73.75 | all-reduce | flops 131072 | bytes 786432 | tf_op jit(solution)/shard_map/psum | solution.py:201
  1396.8 10.8 all_to_all.6
  1409.6 12.5 all-reduce
  1426.7 64.2 %reduce-scatter.8.cloned.1.call-done = f32[2,16,8]{1,2,0:T(8,128)} async-done(((f32[2,16,128]{1,2,0:T(8,128)}), f32[2,16,8]{1,2,0:T(8,128)}) %reduce-scatter.8.cloned.1.call-update) | async-done | bytes 1040 | tf_op jit(solution)/shard_map/reduce_scatter | solution.py:331
  1492.3 74.0 %reduce-scatter.10.cloned.1.call-done = f32[64,32]{1,0:T(8,128)} async-done(((f32[1024,32]{1,0:T(8,128)}), f32[64,32]{1,0:T(8,128)}) %reduce-scatter.10.cloned.1.call-update) | async-done | bytes 8208
  1568.7 66.1 %all-reduce.1 = (f32[]{:T(128)}, f32[2,2]{0,1:T(2,128)S(1)}, f32[2,2]{0,1:T(2,128)S(1)}) all-reduce(f32[]{:T(128)S(6)} %div.320, f32[2,2]{0,1:T(2,128)S(1)} %pad_maximum_fusion.2, f32[2,2]{0,1:T(2,128)S(1)} %maximum_multiply_fusion.8), channel_id=1, replica_groups=mesh['dp'=16,'head'=8] {'dp','head'}, use_global_device_ids=true, to_apply=%region_45.47 | all-reduce | flops 9 | bytes 72 | tf_op jit(solution)/shard_map/psum | solution.py:358
  (611 shorter events, 159.5 us)
Async XLA Ops:
  7.2 770.4 %copy-start = (bf16[512,1024]{1,0:T(8,128)(2,1)S(1)}, bf16[512,1024]{1,0:T(8,128)(2,1)}, u32[]{:S(2)}) copy-start(bf16[512,1024]{1,0:T(8,128)(2,1)} %param.31) | copy-start | bytes 3145732
  7.2 20.9 %copy-start.1 = (bf16[3144,128]{1,0:T(8,128)(2,1)S(1)}, bf16[3144,128]{1,0:T(8,128)(2,1)}, u32[]{:S(2)}) copy-start(bf16[3144,128]{1,0:T(8,128)(2,1)} %param.26) | copy-start | bytes 2414596
  7.2 411.8 %reduce-scatter.6.cloned.1.call-start = ((), (), s32[]{:S(2)}) async-start(), calls=%async_computation.4 | async-start | bytes 17825792 | tf_op jit(solution)/shard_map/reduce_scatter | solution.py:283
  303.3 172.0 %all-gather.2.cloned.1.call-start = ((), (), s32[]{:S(2)}) async-start(), calls=%async_computation.5 | async-start | bytes 9437184 | tf_op jit(solution)/shard_map/all_gather | solution.py:294
  419.0 345.2 %all-reduce.15.cloned.1.call-start = ((), (), s32[]{:S(2)}) async-start(), calls=%async_computation.10 | async-start | bytes 33554432 | tf_op jit(solution)/shard_map/psum | solution.py:43
  420.7 151.7 %copy-start.88 = (bf16[2,16,128]{2,1,0:T(8,128)(2,1)}, bf16[2,16,128]{2,1,0:T(8,128)(2,1)S(1)}, u32[]{:S(2)}) copy-start(bf16[2,16,128]{2,1,0:T(8,128)(2,1)S(1)} %convert_element_type.351) | copy-start | bytes 24580
  422.0 151.4 %copy-start.111 = (pred[2,512]{1,0:T(4,128)(4,1)}, pred[2,512]{1,0:T(4,128)(4,1)S(1)}, u32[]{:S(2)}) copy-start(pred[2,512]{1,0:T(4,128)(4,1)S(1)} %get-tuple-element.137) | copy-start | bytes 3076
  500.9 19.8 %copy-start.32 = (f32[2,512,1024]{2,1,0:T(8,128)}, f32[2,512,1024]{2,1,0:T(8,128)S(1)}, u32[]{:S(2)}) copy-start(f32[2,512,1024]{2,1,0:T(8,128)S(1)} %get-tuple-element.79) | copy-start | bytes 12582916
  523.1 14.8 copy-start.71
  524.8 8.6 copy-start.53
  527.2 7.3 copy-start.49
  542.7 15.3 copy-start.69
  544.4 9.1 copy-start.55
  547.3 7.3 copy-start.51
  580.3 417.5 %all-reduce.13.cloned.1.call-start = ((), (), s32[]{:S(2)}) async-start(), calls=%async_computation.9 | async-start | bytes 33554432 | tf_op jit(solution)/shard_map/psum | solution.py:43
  764.3 4.7 copy-start.48
  768.4 5.0 copy-start.26
  777.5 6.8 copy-start.160
  784.4 6.7 copy-start.29
  784.4 6.7 copy-start.47
  794.9 6.7 copy-start.163
  794.9 6.7 copy-start.28
  794.9 6.7 copy-start.46
  813.5 462.4 %all-reduce.11.cloned.1.call-start = ((), (), s32[]{:S(2)}) async-start(), calls=%async_computation.8 | async-start | bytes 33554432 | tf_op jit(solution)/shard_map/psum | solution.py:146
  1010.1 9.6 copy-start.2
  1010.1 9.6 copy-start.6
  1010.1 17.6 %copy-start.4 = (f32[1024,1024]{1,0:T(8,128)}, f32[1024,1024]{1,0:T(8,128)S(1)}, u32[]{:S(2)}) copy-start(f32[1024,1024]{1,0:T(8,128)S(1)} %get-tuple-element.121) | copy-start | bytes 12582916
  1010.1 17.6 %copy-start.8 = (f32[1024,1024]{1,0:T(8,128)}, f32[1024,1024]{1,0:T(8,128)S(1)}, u32[]{:S(2)}) copy-start(f32[1024,1024]{1,0:T(8,128)S(1)} %get-tuple-element.125) | copy-start | bytes 12582916
  1012.7 4.3 copy-start.158
  1091.6 399.3 %reduce-scatter.8.cloned.1.call-start = ((), (), s32[]{:S(2)}) async-start(), calls=%async_computation.6 | async-start | bytes 139264 | tf_op jit(solution)/shard_map/reduce_scatter | solution.py:331
  1275.9 7.9 copy-start.27
  1276.0 7.9 copy-start.45
  1290.2 53.7 %copy-start.78 = (bf16[2,2,64,512]{3,2,1,0:T(8,128)(2,1)}, bf16[2,2,64,512]{3,2,1,0:T(8,128)(2,1)S(1)}, u32[]{:S(2)}) copy-start(bf16[2,2,64,512]{3,2,1,0:T(8,128)(2,1)S(1)} %convolution_convert_fusion) | copy-start | bytes 786436
  1290.2 5.0 copy-start.25
  1307.6 40.5 %copy-start.80 = (bf16[2,2,64,512]{3,2,1,0:T(8,128)(2,1)}, bf16[2,2,64,512]{3,2,1,0:T(8,128)(2,1)S(1)}, u32[]{:S(2)}) copy-start(bf16[2,2,64,512]{3,2,1,0:T(8,128)(2,1)S(1)} %convolution_convert_fusion.1) | copy-start | bytes 786436
  1307.6 5.1 copy-start.23
  1324.9 27.4 %copy-start.82 = (bf16[2,2,64,512]{3,2,1,0:T(8,128)(2,1)}, bf16[2,2,64,512]{3,2,1,0:T(8,128)(2,1)S(1)}, u32[]{:S(2)}) copy-start(bf16[2,2,64,512]{3,2,1,0:T(8,128)(2,1)S(1)} %convolution_convert_fusion.2) | copy-start | bytes 786436
  1324.9 5.1 copy-start.21
  1342.2 13.8 copy-start.84
  1358.9 32.7 %copy-start.38 = (bf16[2,512,1024]{2,1,0:T(8,128)(2,1)S(1)}, bf16[2,512,1024]{2,1,0:T(8,128)(2,1)}, u32[]{:S(2)}) copy-start(bf16[2,512,1024]{2,1,0:T(8,128)(2,1)} %get-tuple-element.84) | copy-start | bytes 6291460
  1423.1 143.2 %reduce-scatter.10.cloned.1.call-start = ((), (), s32[]{:S(2)}) async-start(), calls=%async_computation.7 | async-start | bytes 557056
  1423.2 67.7 %copy-start.122 = (f32[2,16,8]{1,2,0:T(8,128)S(1)}, f32[2,16,8]{1,2,0:T(8,128)}, u32[]{:S(2)}) copy-start(f32[2,16,8]{1,2,0:T(8,128)} %copy.338) | copy-start | bytes 3076
  1423.2 67.7 %copy-start.153 = (f32[2,16,8]{1,2,0:T(8,128)S(1)}, f32[2,16,8]{1,2,0:T(8,128)}, u32[]{:S(2)}) copy-start(f32[2,16,8]{1,2,0:T(8,128)} %param.42) | copy-start | bytes 3076
  1423.2 67.7 %copy-start.154 = (f32[2,16,8]{1,2,0:T(8,128)S(1)}, f32[2,16,8]{1,2,0:T(8,128)}, u32[]{:S(2)}) copy-start(f32[2,16,8]{1,2,0:T(8,128)} %param.40) | copy-start | bytes 3076
  1423.2 67.7 %copy-start.155 = (f32[2,16,8]{1,2,0:T(8,128)S(1)}, f32[2,16,8]{1,2,0:T(8,128)}, u32[]{:S(2)}) copy-start(f32[2,16,8]{1,2,0:T(8,128)} %param.39) | copy-start | bytes 3076
  1424.7 142.5 %copy-start.145 = (f32[2,64,16]{1,2,0:T(8,128)S(1)}, f32[2,64,16]{1,2,0:T(8,128)}, u32[]{:S(2)}) copy-start(f32[2,64,16]{1,2,0:T(8,128)} %param.41) | copy-start | bytes 24580
  1424.7 142.5 %copy-start.146 = (f32[2,64,16]{1,2,0:T(8,128)S(1)}, f32[2,64,16]{1,2,0:T(8,128)}, u32[]{:S(2)}) copy-start(f32[2,64,16]{1,2,0:T(8,128)} %param.38) | copy-start | bytes 24580
  1424.7 142.5 %copy-start.147 = (f32[2,64,16]{1,2,0:T(8,128)S(1)}, f32[2,64,16]{1,2,0:T(8,128)}, u32[]{:S(2)}) copy-start(f32[2,64,16]{1,2,0:T(8,128)} %param.37) | copy-start | bytes 24580
  (123 other events, 271.6 us)
Sparse Core Ops, SparseCore 0:
  303.4 115.5 reduce-scatter.5
  420.7 54.6 all-gather.1
  580.4 183.7 all-reduce.14
  813.6 184.1 all-reduce.12
  1091.7 184.2 all-reduce.10
  1423.2 67.6 reduce-scatter.7
  1494.4 71.8 reduce-scatter.9
where the time goes:
time: 1650 us
  waiting for transfers between devices  846 us (51%)
  local copies, waits for them, and re-layouts  291 us (18%)
  matrix products  177 us (11%)
  other arithmetic  169 us (10%)
  blocking collectives  139 us (8%)
  between operations  24.4 us (1%)
    psum x2, waiting for transfers between devices, branch_add(): total = lax.psum(partial_out, 'head')  367 us
    gather x1, local copies, waits for them, and re-layouts, per_device(): jnp.take(token_embedding_table, jnp.clip(ids_here, 0, vocab_local - 1), a...  229 us
    psum x1, waiting for transfers between devices, layer_forward(): d_one = d_sum_two + lax.psum(back_part, 'head')  173 us
    reduce_scatter x1, waiting for transfers between devices, per_device(): lax.psum_scatter(jnp.where(inside[:, None], picked.astype(jnp.float32), 0...  116 us
    unnamed x8, waiting for transfers between devices  74.1 us
    psum x1, blocking collectives, per_device(): lax.psum((sq_down, sq_up, loss_part), ('dp', 'head'))  66.1 us
    reduce_scatter x1, waiting for transfers between devices, per_device(): lax.psum_scatter(sum_up, 'dp', scatter_dimension=2, tiled=True)  64.2 us
    all_gather x1, waiting for transfers between devices, per_device(): tokens = lax.all_gather(columns, 'head', axis=1, tiled=True)  51.6 us
  transfers between devices with their start and end apart: 7, of which 7 were waited for; matrix products, arithmetic and copies ran while one was open for 1% of the time, Pallas kernels for 0%

commit v1 on v0

--- a/solution.py
+++ b/solution.py
@@ -17,6 +17,28 @@
 learn_rate = 0.25
 norm_eps = 1e-05
 contract_last = (((1,), (1,)), ((), ()))
+
+
+def joined_along(blocks, dim):
+    blocks = jnp.moveaxis(blocks, 0, dim)
+    shape = blocks.shape
+    return blocks.reshape(*shape[:dim], shape[dim] * shape[dim + 1], *shape[dim + 2 :])
+
+
+def gather_around(value, axis, dim):
+    size = lax.axis_size(axis)
+    pairs = [(i, (i + 1) % size) for i in range(size)]
+    back = [(b, a) for a, b in pairs]
+    lower, upper = ([], [])
+    for step in range(size - 1):
+        if step % 2 == 0:
+            lower.append(lax.ppermute(lower[-1] if lower else value, axis, pairs))
+        else:
+            upper.append(lax.ppermute(upper[-1] if upper else value, axis, back))
+    blocks = jnp.stack([*lower[::-1], value, *upper])
+    shift = lax.axis_index(axis) - len(lower)
+    blocks = blocks[(jnp.arange(size) - shift) % size]
+    return joined_along(blocks, dim)
 
 
 def gelu_exact(inputs):
@@ -291,7 +313,7 @@
     down_pair = jnp.concatenate([down_reduced[0], down_reduced[1]], 1)
     micro_examples = ex_dev // MICRO
     own_share = ex_dev // n_head
-    tokens = lax.all_gather(columns, "head", axis=1, tiled=True)
+    tokens = gather_around(columns, "head", 1)
     hidden_all, unused_std = norm_rows(
         tokens.astype(jnp.float32).reshape(ex_dev, sequence_length, width) + pos_f,
         layer_norm_gains[0],

time: 1650 us -> 1740 us (1.055)
  local copies, waits for them, and re-layouts: 291 us -> 360 us
  other arithmetic: 169 us -> 190 us
    all_gather x1 -> x0, waiting for transfers between devices: 51.6 us -> none  [per_device(): tokens = lax.all_gather(columns, 'head', axis=1, tiled=True)]
    convert_element_type x0 -> x2, local copies, waits for them, and re-layouts: none -> 36 us  [per_device(): tokens.astype(jnp.float32).reshape(ex_dev, sequence_length, width) + pos_f]
    ppermute x0 -> x7, waiting for transfers between devices: none -> 34.8 us  [the longest x4 34.4 us: gather_around(): lower.append(lax.ppermute(lower[-1] if lower else value, axis, pairs))]
    unnamed x358 -> x380, local copies, waits for them, and re-layouts: 30.4 us -> 53.3 us
    unnamed x8 -> x7, waiting for transfers between devices: 74.1 us -> 74 us
  transfers between devices with their start and end apart: 7 -> 13, of which waited for: 7 -> 10; matrix products, arithmetic and copies ran while one was open for 1% -> 2% of each run, Pallas kernels for 0% -> 0%
where the time goes in v1:
time: 1740 us; the launch traced here: 1730 us
  waiting for transfers between devices  830 us (48%)
  local copies, waits for them, and re-layouts  360 us (21%)
  other arithmetic  190 us (11%)
  matrix products  178 us (10%)
  blocking collectives  139 us (8%)
  between operations  24.5 us (1%)
    psum x2, waiting for transfers between devices, branch_add(): total = lax.psum(partial_out, 'head')  368 us
    gather x1, local copies, waits for them, and re-layouts, per_device(): jnp.take(token_embedding_table, jnp.clip(ids_here, 0, vocab_local - 1), a...  227 us
    psum x1, waiting for transfers between devices, layer_forward(): d_one = d_sum_two + lax.psum(back_part, 'head')  173 us
    reduce_scatter x1, waiting for transfers between devices, per_device(): lax.psum_scatter(jnp.where(inside[:, None], picked.astype(jnp.float32), 0...  116 us
    unnamed x7, waiting for transfers between devices  74 us
    psum x1, blocking collectives, per_device(): lax.psum((sq_down, sq_up, loss_part), ('dp', 'head'))  66 us
    reduce_scatter x1, waiting for transfers between devices, per_device(): lax.psum_scatter(sum_up, 'dp', scatter_dimension=2, tiled=True)  64.1 us
    unnamed x380, local copies, waits for them, and re-layouts  53.3 us
  transfers between devices with their start and end apart: 13, of which 10 were waited for; matrix products, arithmetic and copies ran while one was open for 2% of the time, Pallas kernels for 0%

profile of v1, /device:TPU:1, one launch (start us, length us, event | category | flops | bytes accessed | tf_op | source)
XLA Modules:
  0.0 1734.5 jit_solution(10301829808593857820)
XLA Ops:
  7.3 19.8 %all_gather.6 = s32[128,512]{1,0:T(8,128)S(1)} all-gather(s32[8,512]{1,0:T(8,128)} %param.22), channel_id=1, replica_groups=mesh['dp'=16,'head'=8] {'dp'}, dimensions={0}, use_global_device_ids=true | all-gather | bytes 278528 | tf_op jit(solution)/shard_map/all_gather | solution.py:299
  28.1 227.3 %gather_fusion = bf16[65536,128]{1,0:T(8,128)(2,1)} fusion(bf16[3144,128]{1,0:T(8,128)(2,1)S(1)} %copy-done.1, s32[65536]{0:T(1024)S(1)} %broadcast_clamp_fusion), kind=kCustom, calls=%fused_computation | custom fusion | bytes 33816576 | tf_op jit(solution)/shard_map/jit(_take)/gather | solution.py:304
  255.3 46.3 %select_convert_fusion = bf16[65536,128]{1,0:T(8,128)(2,1)} fusion(bf16[65536,128]{1,0:T(8,128)(2,1)} %gather_fusion, pred[65536]{0:T(1024)(128)(4,1)S(1)} %compare_and_fusion, pred[65536]{0:T(1024)(128)(4,1)S(1)} %bitcast.578), kind=kLoop, calls=%fused_computation.2 | loop fusion | flops 33554432 | bytes 33685504 | tf_op jit(solution)/shard_map/convert_element_type | solution.py:306
  301.7 115.7 %reduce-scatter.6.cloned.1.call-done = bf16[4096,128]{1,0:T(8,128)(2,1)} async-done(((bf16[65536,128]{1,0:T(8,128)(2,1)}), bf16[4096,128]{1,0:T(8,128)(2,1)}) %reduce-scatter.6.cloned.1.call-update) | async-done | bytes 1048592 | tf_op jit(solution)/shard_map/reduce_scatter | solution.py:305
  419.6 12.1 collective-permute-done
  435.1 11.6 collective-permute-done.1
  450.8 10.7 collective-permute-done.2
  467.7 8.3 copy.352
  495.8 8.1 gather_fusion.1
  503.9 10.5 convert_bitcast_fusion
  514.4 11.5 fusion
  525.9 9.8 multiply_reduce_fusion
  535.6 17.8 %copy.184 = f32[4096,8,128]{2,1,0:T(8,128)} copy(f32[4096,8,128]{2,0,1:T(8,128)} %convert_bitcast_fusion) | data formatting | bytes 33554432 | tf_op jit(solution)/shard_map/convert_element_type | solution.py:318
  553.4 18.2 %reshape.710 = f32[8,512,1024]{2,1,0:T(8,128)} reshape(f32[4096,8,128]{2,1,0:T(8,128)} %copy.184) | data formatting | bytes 33554432 | tf_op jit(solution)/shard_map/convert_element_type | solution.py:318
  571.7 7.8 multiply_add_fusion
  579.5 3.7 fusion.386
  583.1 4.8 fusion.385
  588.0 3.9 fusion.183
  667.6 184.2 %all-reduce.15.cloned.1.call-done = (f32[1024,1024]{1,0:T(8,128)}, f32[1024,1024]{1,0:T(8,128)}, f32[1024,1024]{1,0:T(8,128)}, f32[1024,1024]{1,0:T(8,128)}) async-done(((f32[1024,1024]{1,0:T(8,128)}, f32[1024,1024]{1,0:T(8,128)}, f32[1024,1024]{1,0:T(8,128)}, f32[1024,1024]{1,0:T(8,128)}), (f32[1024,1024]{1,0:T(8,128)}, f32[1024,1024]{1,0:T(8,128)}, f32[1024,1024]{1,0:T(8,128)}, ...) | async-done | bytes 16777232 | tf_op jit(solution)/shard_map/psum | solution.py:65
  851.9 4.1 fusion.384
  865.2 6.8 fusion.140
  872.0 6.7 fusion.138
  882.6 6.7 fusion.139
  894.5 6.6 fusion.137
  902.1 183.4 %all-reduce.13.cloned.1.call-done = (f32[1024,1024]{1,0:T(8,128)}, f32[1024,1024]{1,0:T(8,128)}, f32[1024,1024]{1,0:T(8,128)}, f32[1024,1024]{1,0:T(8,128)}) async-done(((f32[1024,1024]{1,0:T(8,128)}, f32[1024,1024]{1,0:T(8,128)}, f32[1024,1024]{1,0:T(8,128)}, f32[1024,1024]{1,0:T(8,128)}), (f32[1024,1024]{1,0:T(8,128)}, f32[1024,1024]{1,0:T(8,128)}, f32[1024,1024]{1,0:T(8,128)}, ...) | async-done | bytes 16777232 | tf_op jit(solution)/shard_map/psum | solution.py:65
  1085.5 12.5 fusion.373
  1100.6 4.3 multiply_reduce_fusion.13
  1107.6 5.7 fusion.24
  1115.6 8.7 fusion.18
  1124.3 10.9 fusion.144
  1135.2 3.9 fusion.31
  1139.1 11.0 fusion.143
  1150.2 7.4 fusion.29
  1157.5 11.0 fusion.142
  1168.5 10.8 fusion.141
  1190.3 173.4 %all-reduce.11.cloned.1.call-done = (f32[1024,1024]{1,0:T(8,128)}, f32[1024,1024]{1,0:T(8,128)}, f32[1024,1024]{1,0:T(8,128)}, f32[1024,1024]{1,0:T(8,128)}) async-done(((f32[1024,1024]{1,0:T(8,128)}, f32[1024,1024]{1,0:T(8,128)}, f32[1024,1024]{1,0:T(8,128)}, f32[1024,1024]{1,0:T(8,128)}), (f32[1024,1024]{1,0:T(8,128)}, f32[1024,1024]{1,0:T(8,128)}, f32[1024,1024]{1,0:T(8,128)}, ...) | async-done | bytes 16777232 | tf_op jit(solution)/shard_map/psum | solution.py:168
  1363.8 7.6 fusion.372
  1382.8 5.9 fusion.371
  1395.1 3.5 multiply_reduce_fusion.4
  1400.2 5.9 fusion.370
  1412.5 3.7 multiply_reduce_fusion.7
  1417.5 5.9 fusion.369
  1447.3 29.8 %all-reduce.16 = (bf16[1024,32]{0,1:T(8,128)(2,1)}, bf16[1024,32]{0,1:T(8,128)(2,1)}, bf16[1024,32]{0,1:T(8,128)(2,1)}, bf16[1024,32]{0,1:T(8,128)(2,1)}) all-reduce(f32[1024,32]{0,1:T(8,128)S(1)} %maximum_multiply_fusion.3, f32[1024,32]{0,1:T(8,128)} %maximum_multiply_fusion.2, ...), channel_id=1, replica_groups=mesh['dp'=16,'head'=8] {'head'}, use_global_device_ids=true, to_apply=%region_73.75 | all-reduce | flops 131072 | bytes 786432 | tf_op jit(solution)/shard_map/psum | solution.py:223
  1484.4 10.8 all_to_all.6
  1497.3 12.5 all-reduce
  1514.4 64.1 %reduce-scatter.8.cloned.1.call-done = f32[2,16,8]{1,2,0:T(8,128)} async-done(((f32[2,16,128]{1,2,0:T(8,128)}), f32[2,16,8]{1,2,0:T(8,128)}) %reduce-scatter.8.cloned.1.call-update) | async-done | bytes 1040 | tf_op jit(solution)/shard_map/reduce_scatter | solution.py:353
  1579.9 73.9 %reduce-scatter.10.cloned.1.call-done = f32[64,32]{1,0:T(8,128)} async-done(((f32[1024,32]{1,0:T(8,128)}), f32[64,32]{1,0:T(8,128)}) %reduce-scatter.10.cloned.1.call-update) | async-done | bytes 8208
  1656.2 66.0 %all-reduce.1 = (f32[]{:T(128)}, f32[2,2]{0,1:T(2,128)S(1)}, f32[2,2]{0,1:T(2,128)S(1)}) all-reduce(f32[]{:T(128)S(6)} %div.320, f32[2,2]{0,1:T(2,128)S(1)} %pad_maximum_fusion.2, f32[2,2]{0,1:T(2,128)S(1)} %maximum_multiply_fusion.8), channel_id=1, replica_groups=mesh['dp'=16,'head'=8] {'dp','head'}, use_global_device_ids=true, to_apply=%region_45.47 | all-reduce | flops 9 | bytes 72 | tf_op jit(solution)/shard_map/psum | solution.py:380
  (653 shorter events, 214.8 us)
Async XLA Ops:
  7.2 858.0 %copy-start = (bf16[512,1024]{1,0:T(8,128)(2,1)S(1)}, bf16[512,1024]{1,0:T(8,128)(2,1)}, u32[]{:S(2)}) copy-start(bf16[512,1024]{1,0:T(8,128)(2,1)} %param.31) | copy-start | bytes 3145732
  7.2 20.9 %copy-start.1 = (bf16[3144,128]{1,0:T(8,128)(2,1)S(1)}, bf16[3144,128]{1,0:T(8,128)(2,1)}, u32[]{:S(2)}) copy-start(bf16[3144,128]{1,0:T(8,128)(2,1)} %param.26) | copy-start | bytes 2414596
  7.2 410.2 %reduce-scatter.6.cloned.1.call-start = ((), (), s32[]{:S(2)}) async-start(), calls=%async_computation.4 | async-start | bytes 17825792 | tf_op jit(solution)/shard_map/reduce_scatter | solution.py:305
  301.6 147.8 %copy-start.153 = (s32[8]{0:T(128)S(1)}, s32[8]{0:T(128)}, u32[]{:S(2)}) copy-start(s32[8]{0:T(128)} %param.23) | copy-start | bytes 100
  301.6 162.3 %copy-start.45 = (bf16[512,1024]{1,0:T(8,128)(2,1)S(1)}, bf16[512,1024]{1,0:T(8,128)(2,1)}, u32[]{:S(2)}) copy-start(bf16[512,1024]{1,0:T(8,128)(2,1)} %param.27) | copy-start | bytes 3145732
  301.6 550.2 %all-reduce.15.cloned.1.call-start = ((), (), s32[]{:S(2)}) async-start(), calls=%async_computation.9 | async-start | bytes 33554432 | tf_op jit(solution)/shard_map/psum | solution.py:65
  417.4 14.3 collective-permute-start
  432.7 14.1 collective-permute-start.1
  435.0 14.8 collective-permute-start.4
  446.8 14.6 collective-permute-start.2
  449.4 26.6 %copy-start.125 = (pred[8,512]{1,0:T(8,128)(4,1)}, pred[8,512]{1,0:T(8,128)(4,1)S(1)}, u32[]{:S(2)}) copy-start(pred[8,512]{1,0:T(8,128)(4,1)S(1)} %iota_compare_fusion) | copy-start | bytes 12292
  449.9 28.7 %collective-permute-start.5 = (bf16[4096,128]{1,0:T(8,128)(2,1)}, bf16[4096,128]{1,0:T(8,128)(2,1)}, u32[]{:S(2)}, u32[]{:S(2)}) collective-permute-start(bf16[4096,128]{1,0:T(8,128)(2,1)} %collective-permute-done.4), channel_id=1, source_target_pairs={{1,0},{2,1},{3,2},{4,3},{5,4},{6,5},{7,6},{0,7},{9,8},{10,9},{11,1... | collective-permute-start | bytes 3145736 | tf_op jit(solution)/shard_map/ppermute | solution.py:37
  461.4 19.6 %collective-permute-start.3 = (bf16[4096,128]{1,0:T(8,128)(2,1)}, bf16[4096,128]{1,0:T(8,128)(2,1)}, u32[]{:S(2)}, u32[]{:S(2)}) collective-permute-start(bf16[4096,128]{1,0:T(8,128)(2,1)} %collective-permute-done.2), channel_id=1, source_target_pairs={{0,1},{1,2},{2,3},{3,4},{4,5},{5,6},{6,7},{7,0},{8,9},{9,10},{10,1... | collective-permute-start | bytes 3145736 | tf_op jit(solution)/shard_map/ppermute | solution.py:35
  467.6 8.4 copy-start.107
  467.7 8.4 copy-start.142
  467.7 9.1 copy-start.155
  467.7 9.6 copy-start.156
  476.1 183.6 %copy-start.93 = (bf16[2,16,128]{2,1,0:T(8,128)(2,1)}, bf16[2,16,128]{2,1,0:T(8,128)(2,1)S(1)}, u32[]{:S(2)}) copy-start(bf16[2,16,128]{2,1,0:T(8,128)(2,1)S(1)} %convert_element_type.366) | copy-start | bytes 24580
  476.7 183.9 %copy-start.116 = (pred[2,512]{1,0:T(4,128)(4,1)}, pred[2,512]{1,0:T(4,128)(4,1)S(1)}, u32[]{:S(2)}) copy-start(pred[2,512]{1,0:T(4,128)(4,1)S(1)} %get-tuple-element.137) | copy-start | bytes 3076
  478.5 16.2 collective-permute-start.6
  503.9 21.9 %slice-start = ((s8[8388608]{0:T(1024)(128)(4,1)}), s8[4194304]{0:T(1024)(128)(4,1)S(1)}, s32[]{:S(2)}) async-start(s8[8388608]{0:T(1024)(128)(4,1)} %bitcast.498), calls=%async_computation.10 | async-start | bytes 8388608
  514.4 11.5 slice-start.1
  553.4 18.2 %copy-start.43 = (f32[512,1024]{1,0:T(8,128)S(1)}, f32[512,1024]{1,0:T(8,128)}, u32[]{:S(2)}) copy-start(f32[512,1024]{1,0:T(8,128)} %convert_element_type.359) | copy-start | bytes 6291460
  588.0 19.7 %copy-start.32 = (f32[2,512,1024]{2,1,0:T(8,128)}, f32[2,512,1024]{2,1,0:T(8,128)S(1)}, u32[]{:S(2)}) copy-start(f32[2,512,1024]{2,1,0:T(8,128)S(1)} %get-tuple-element.79) | copy-start | bytes 12582916
  610.1 15.0 copy-start.73
  611.8 8.3 copy-start.55
  629.9 15.2 copy-start.71
  631.6 9.1 copy-start.57
  667.6 417.9 %all-reduce.13.cloned.1.call-start = ((), (), s32[]{:S(2)}) async-start(), calls=%async_computation.8 | async-start | bytes 33554432 | tf_op jit(solution)/shard_map/psum | solution.py:65
  901.2 462.6 %all-reduce.11.cloned.1.call-start = ((), (), s32[]{:S(2)}) async-start(), calls=%async_computation.7 | async-start | bytes 33554432 | tf_op jit(solution)/shard_map/psum | solution.py:168
  1097.9 9.6 copy-start.2
  1097.9 9.6 copy-start.6
  1098.0 17.6 %copy-start.4 = (f32[1024,1024]{1,0:T(8,128)}, f32[1024,1024]{1,0:T(8,128)S(1)}, u32[]{:S(2)}) copy-start(f32[1024,1024]{1,0:T(8,128)S(1)} %get-tuple-element.121) | copy-start | bytes 12582916
  1098.0 17.6 %copy-start.8 = (f32[1024,1024]{1,0:T(8,128)}, f32[1024,1024]{1,0:T(8,128)S(1)}, u32[]{:S(2)}) copy-start(f32[1024,1024]{1,0:T(8,128)S(1)} %get-tuple-element.125) | copy-start | bytes 12582916
  1179.4 399.1 %reduce-scatter.8.cloned.1.call-start = ((), (), s32[]{:S(2)}) async-start(), calls=%async_computation.5 | async-start | bytes 139264 | tf_op jit(solution)/shard_map/reduce_scatter | solution.py:353
  1377.8 53.7 %copy-start.83 = (bf16[2,2,64,512]{3,2,1,0:T(8,128)(2,1)}, bf16[2,2,64,512]{3,2,1,0:T(8,128)(2,1)S(1)}, u32[]{:S(2)}) copy-start(bf16[2,2,64,512]{3,2,1,0:T(8,128)(2,1)S(1)} %convolution_convert_fusion) | copy-start | bytes 786436
  1395.1 40.5 %copy-start.85 = (bf16[2,2,64,512]{3,2,1,0:T(8,128)(2,1)}, bf16[2,2,64,512]{3,2,1,0:T(8,128)(2,1)S(1)}, u32[]{:S(2)}) copy-start(bf16[2,2,64,512]{3,2,1,0:T(8,128)(2,1)S(1)} %convolution_convert_fusion.1) | copy-start | bytes 786436
  1412.4 27.4 %copy-start.87 = (bf16[2,2,64,512]{3,2,1,0:T(8,128)(2,1)}, bf16[2,2,64,512]{3,2,1,0:T(8,128)(2,1)S(1)}, u32[]{:S(2)}) copy-start(bf16[2,2,64,512]{3,2,1,0:T(8,128)(2,1)S(1)} %convolution_convert_fusion.2) | copy-start | bytes 786436
  1429.8 13.8 copy-start.89
  1446.5 32.8 %copy-start.38 = (bf16[2,512,1024]{2,1,0:T(8,128)(2,1)S(1)}, bf16[2,512,1024]{2,1,0:T(8,128)(2,1)}, u32[]{:S(2)}) copy-start(bf16[2,512,1024]{2,1,0:T(8,128)(2,1)} %get-tuple-element.84) | copy-start | bytes 6291460
  1510.8 143.0 %reduce-scatter.10.cloned.1.call-start = ((), (), s32[]{:S(2)}) async-start(), calls=%async_computation.6 | async-start | bytes 557056
  1510.8 67.7 %copy-start.127 = (f32[2,16,8]{1,2,0:T(8,128)S(1)}, f32[2,16,8]{1,2,0:T(8,128)}, u32[]{:S(2)}) copy-start(f32[2,16,8]{1,2,0:T(8,128)} %copy.344) | copy-start | bytes 3076
  1510.8 67.7 %copy-start.158 = (f32[2,16,8]{1,2,0:T(8,128)S(1)}, f32[2,16,8]{1,2,0:T(8,128)}, u32[]{:S(2)}) copy-start(f32[2,16,8]{1,2,0:T(8,128)} %param.42) | copy-start | bytes 3076
  1510.8 67.7 %copy-start.159 = (f32[2,16,8]{1,2,0:T(8,128)S(1)}, f32[2,16,8]{1,2,0:T(8,128)}, u32[]{:S(2)}) copy-start(f32[2,16,8]{1,2,0:T(8,128)} %param.40) | copy-start | bytes 3076
  1510.8 67.7 %copy-start.160 = (f32[2,16,8]{1,2,0:T(8,128)S(1)}, f32[2,16,8]{1,2,0:T(8,128)}, u32[]{:S(2)}) copy-start(f32[2,16,8]{1,2,0:T(8,128)} %param.39) | copy-start | bytes 3076
  1512.4 142.4 %copy-start.150 = (f32[2,64,16]{1,2,0:T(8,128)S(1)}, f32[2,64,16]{1,2,0:T(8,128)}, u32[]{:S(2)}) copy-start(f32[2,64,16]{1,2,0:T(8,128)} %param.41) | copy-start | bytes 24580
  1512.4 142.4 %copy-start.151 = (f32[2,64,16]{1,2,0:T(8,128)S(1)}, f32[2,64,16]{1,2,0:T(8,128)}, u32[]{:S(2)}) copy-start(f32[2,64,16]{1,2,0:T(8,128)} %param.38) | copy-start | bytes 24580
  1512.4 142.3 %copy-start.152 = (f32[2,64,16]{1,2,0:T(8,128)S(1)}, f32[2,64,16]{1,2,0:T(8,128)}, u32[]{:S(2)}) copy-start(f32[2,64,16]{1,2,0:T(8,128)} %param.37) | copy-start | bytes 24580
  (136 other events, 368.9 us)
Sparse Core Ops, SparseCore 0:
  301.8 115.5 reduce-scatter.5
  667.7 184.1 all-reduce.14
  901.3 184.1 all-reduce.12
  1179.5 184.1 all-reduce.10
  1510.9 67.5 reduce-scatter.7
  1581.9 71.8 reduce-scatter.9
